TPU v7x, 32 devices: a whole 2x2x4 slice. The times are simulated.
32 devices in a mesh: dp: 4 (over y, core), tensor: 8 (over z, x).
Axes of the slice: x: 2, y: 2, z: 4, core: 2. Of those that a mesh axis runs over, the one named last changes fastest.
Arguments:
- tokens: bfloat16 [3072, 8192], P('dp', 'tensor'), may hold values from -6 to 6
- cotangent: bfloat16 [3072, 512], P('dp', 'tensor'), may hold values from -0.0625 to 0.0625
- frozen_value_weight: bfloat16 [8192, 512], P('tensor'), may hold values from -0.0625 to 0.0625
- adapter_down_weight: bfloat16 [8, 32, 8192], P('tensor'), may hold values from -0.0625 to 0.0625
- adapter_up_weight: bfloat16 [8, 32, 512], P('tensor'), may hold values from -1 to 1
- member: int32 [24, 1], P('dp'), may hold values from 0 to 7; in each aligned block of 6 rows (0 to 5, 6 to 11, ...) at most 2 rows name the same one
Outputs:
- output: bfloat16 [3072, 512], P(('dp', 'tensor'))
- grad_down: float32 [8, 32, 8192], P('tensor', None, 'dp')
- grad_up: float32 [8, 32, 512], P('tensor', 'dp')
Inputs may be any that keep to these rules, and one draw needn't show every extreme that they name: Within the 6 blocks of one data index no member appears more than 2 times, and some member appears exactly 2 times there.
All inputs are finite; a program needn't handle non-finite values.
Results may differ from a plain program's by a relative error of at most 0.015.
Values may be sent and summed in bfloat16 or wider, within the bound.
A program may use at most 64 MiB of HBM per device.

v0:
```python
import jax
import jax.numpy as jnp
from jax import lax
from jax.sharding import PartitionSpec as P

BLK = 128
CAP = 2


adapter_scale = 2.0
contract_trailing = (((1,), (1,)), ((), ()))
contract_leading = (((0,), (0,)), ((), ()))


def slot_table(member_ids, tensor_size):
    block_total = member_ids.shape[0]
    position = jnp.arange(block_total, dtype=jnp.int32)
    same_member = member_ids[:, None] == member_ids[None, :]
    earlier = position[None, :] < position[:, None]
    slot_rank = jnp.sum(jnp.logical_and(same_member, earlier), axis=1)
    owners = jnp.arange(tensor_size, dtype=jnp.int32)
    slot_numbers = jnp.arange(CAP, dtype=jnp.int32)
    picked = jnp.logical_and(
        member_ids[None, None, :] == owners[:, None, None],
        slot_rank[None, None, :] == slot_numbers[None, :, None],
    )
    return picked.astype(jnp.bfloat16)


def shards(tokens, cotangent, frozen_value_weight, adapter_down_weight, adapter_up_weight, member):
    tensor_size = lax.axis_size("tensor")
    owner_index = lax.axis_index("tensor")
    row_total = tokens.shape[0]
    feature_width = tokens.shape[1]
    cot_width = cotangent.shape[1]
    out_width = frozen_value_weight.shape[1]
    block_total = row_total // BLK
    own_rows = row_total // tensor_size
    member_ids = member[:, 0]
    picked = slot_table(member_ids, tensor_size)
    flat_picked = picked.reshape(tensor_size * CAP, block_total)
    token_blocks = tokens.reshape(block_total, BLK * feature_width)
    cot_blocks = cotangent.reshape(block_total, BLK * cot_width)
    send_tokens = jnp.dot(flat_picked, token_blocks, preferred_element_type=jnp.float32).astype(
        jnp.bfloat16
    )
    send_tokens = send_tokens.reshape(tensor_size, CAP * BLK, feature_width)
    send_cot = jnp.dot(flat_picked, cot_blocks, preferred_element_type=jnp.float32).astype(
        jnp.bfloat16
    )
    send_cot = send_cot.reshape(tensor_size, CAP * BLK, cot_width)
    got_tokens, got_cot = (
        lax.all_to_all(send_tokens, "tensor", split_axis=0, concat_axis=2, tiled=True),
        lax.all_to_all(send_cot, "tensor", split_axis=0, concat_axis=2, tiled=True),
    )
    slot_tokens = got_tokens[0]
    slot_cot = got_cot[0]
    down_projection = adapter_down_weight[0]
    up_projection = adapter_up_weight[0]
    hidden_state = lax.dot_general(
        slot_tokens, down_projection, contract_trailing, preferred_element_type=jnp.float32
    ).astype(jnp.bfloat16)
    adapter_result = (
        adapter_scale * jnp.dot(hidden_state, up_projection, preferred_element_type=jnp.float32)
    ).astype(jnp.bfloat16)
    backward_projection = (
        adapter_scale
        * lax.dot_general(
            slot_cot, up_projection, contract_trailing, preferred_element_type=jnp.float32
        )
    ).astype(jnp.bfloat16)
    local_down = lax.dot_general(
        backward_projection, slot_tokens, contract_leading, preferred_element_type=jnp.float32
    )
    member_up_weight = adapter_scale * lax.dot_general(
        hidden_state, slot_cot, contract_leading, preferred_element_type=jnp.float32
    )
    base_total = lax.psum_scatter(
        jnp.dot(tokens, frozen_value_weight, preferred_element_type=jnp.float32).astype(
            jnp.bfloat16
        ),
        "tensor",
        scatter_dimension=0,
        tiled=True,
    ).astype(jnp.float32)
    my_slots = lax.dynamic_index_in_dim(picked, owner_index, 0, keepdims=False)
    placed = jnp.dot(
        my_slots.T, adapter_result.reshape(CAP, BLK * out_width), preferred_element_type=jnp.float32
    ).astype(jnp.bfloat16)
    placed = placed.reshape(tensor_size, own_rows, out_width)
    returned = lax.all_to_all(placed, "tensor", split_axis=0, concat_axis=0, tiled=True)
    adapter_rows = jnp.sum(returned.astype(jnp.float32), axis=0)
    output = (base_total + adapter_rows).astype(jnp.bfloat16)
    grad_down, grad_up = (
        lax.psum_scatter(
            local_down[None].astype(jnp.bfloat16), "dp", scatter_dimension=2, tiled=True
        ).astype(jnp.float32),
        lax.psum_scatter(
            member_up_weight[None].astype(jnp.bfloat16), "dp", scatter_dimension=1, tiled=True
        ).astype(jnp.float32),
    )
    return (output, grad_down, grad_up)


def solution(mesh):
    placed = (
        P("dp", "tensor"),
        P("dp", "tensor"),
        P("tensor", None),
        P("tensor", None, None),
        P("tensor", None, None),
        P("dp", None),
    )
    return jax.shard_map(
        shards,
        mesh=mesh,
        in_specs=placed,
        out_specs=(P(("dp", "tensor"), None), P("tensor", None, "dp"), P("tensor", "dp", None)),
        check_vma=False,
    )
```

profile of v0, /device:TPU:0, one launch (start us, length us, event | category | flops | bytes accessed | tf_op | source)
XLA Modules:
  0.0 258.6 jit_solution(10288526673390440713)
XLA Ops:
  7.2 0.8 iota_compare_fusion.1
  7.9 0.9 convert_reduce_fusion.1
  8.9 3.4 %reshape.95 = bf16[6,131072]{1,0:T(8,128)(2,1)S(1)} reshape(bf16[768,1024]{1,0:T(8,128)(2,1)} %param.6) | data formatting | bytes 3145728 | tf_op jit(solution)/shard_map/reshape | solution.py:42
  12.2 3.2 %convolution_convert_fusion = bf16[16,131072]{1,0:T(8,128)(2,1)} fusion(pred[16,6]{1,0:T(8,128)(4,1)S(1)} %and.35, bf16[6,131072]{1,0:T(8,128)(2,1)S(1)} %reshape.95), kind=kOutput, calls=%fused_computation | convolution fusion | flops 27262976 | bytes 5767264 | tf_op jit(solution)/shard_map/dot_general | solution.py:44
  15.5 4.8 %reshape.96 = bf16[8,256,1024]{2,1,0:T(8,128)(2,1)} reshape(bf16[16,131072]{1,0:T(8,128)(2,1)} %convolution_convert_fusion) | data formatting | bytes 8388608 | tf_op jit(solution)/shard_map/reshape | solution.py:47
  20.3 6.5 %copy.15 = bf16[8,256,1024]{1,2,0:T(8,128)(2,1)} copy(bf16[8,256,1024]{2,1,0:T(8,128)(2,1)} %reshape.96) | data formatting | bytes 8388608 | tf_op jit(solution)/shard_map/reshape | solution.py:47
  26.8 7.4 %all-to-all-start = ((bf16[8,256,1024]{1,2,0:T(8,128)(2,1)}), bf16[8,256,1024]{1,2,0:T(8,128)(2,1)}, u32[]{:S(2)}, u32[]{:S(2)}) async-start(bf16[8,256,1024]{1,2,0:T(8,128)(2,1)} %copy.15), calls=%async_computation.1 | async-start | bytes 8388608 | tf_op jit(solution)/shard_map/all_to_all | solution.py:53
  34.2 0.2 copy.16
  34.4 0.2 reshape.99
  34.6 0.2 convolution_convert_fusion.3
  34.8 0.5 reshape.100
  35.3 0.9 copy.17
  36.2 91.2 %all-to-all-done = bf16[8,256,1024]{1,2,0:T(8,128)(2,1)} async-done(((bf16[8,256,1024]{1,2,0:T(8,128)(2,1)}), bf16[8,256,1024]{1,2,0:T(8,128)(2,1)}, u32[]{:S(2)}, u32[]{:S(2)}) %all-to-all-start) | async-done | bytes 4194336 | tf_op jit(solution)/shard_map/all_to_all | solution.py:53
  127.5 3.6 %all-to-all-start.2 = ((bf16[8,256,64]{1,2,0:T(8,128)(2,1)}), bf16[8,256,64]{1,2,0:T(8,128)(2,1)S(1)}, u32[]{:S(2)}, u32[]{:S(2)}) async-start(bf16[8,256,64]{1,2,0:T(8,128)(2,1)} %copy.17), calls=%async_computation.3 | async-start | bytes 524288 | tf_op jit(solution)/shard_map/all_to_all | solution.py:54
  131.2 3.1 %convolution_convert_fusion.5 = bf16[256,32]{0,1:T(8,128)(2,1)S(1)} fusion(bf16[256,8192]{0,1:T(8,128)(2,1)} %bitcast.4, bf16[1,32,8192]{2,1,0:T(8,128)(2,1)S(1)} %copy-done.2), kind=kOutput, calls=%fused_computation.14 | convolution fusion | flops 134225920 | bytes 4734976 | tf_op jit(solution)/shard_map/dot_general | solution.py:60
  134.3 5.9 %all-to-all-done.2 = bf16[8,256,64]{1,2,0:T(8,128)(2,1)S(1)} async-done(((bf16[8,256,64]{1,2,0:T(8,128)(2,1)}), bf16[8,256,64]{1,2,0:T(8,128)(2,1)S(1)}, u32[]{:S(2)}, u32[]{:S(2)}) %all-to-all-start.2) | async-done | bytes 262176 | tf_op jit(solution)/shard_map/all_to_all | solution.py:54
  140.2 0.8 fusion.3
  141.0 0.0 reduce-scatter.6.cloned.1.call-start
  141.1 4.4 %fusion = bf16[1,32,8192]{2,1,0:T(8,128)(2,1)} fusion(bf16[256,8192]{0,1:T(8,128)(2,1)} %bitcast.4, bf16[256,512]{0,1:T(8,128)(2,1)S(1)} %bitcast.41, bf16[1,32,512]{2,1,0:T(8,128)(2,1)S(1)} %copy-done.3), kind=kOutput, calls=%fused_computation.3 | convolution fusion | flops 142884864 | bytes 5013504 | tf_op jit(solution)/shard_map/dot_general | solution.py:72
  145.6 1.9 convolution_convert_fusion.4
  147.5 0.2 fusion.1
  147.7 0.2 reshape.97
  147.9 0.5 convolution_convert_fusion.1
  148.5 2.1 reshape.98
  150.5 3.6 %all-to-all-start.1 = ((bf16[8,96,512]{2,1,0:T(8,128)(2,1)}), bf16[8,96,512]{2,1,0:T(8,128)(2,1)S(1)}, u32[]{:S(2)}, u32[]{:S(2)}) async-start(bf16[8,96,512]{2,1,0:T(8,128)(2,1)} %reshape.98), calls=%async_computation.2 | async-start | bytes 1572864 | tf_op jit(solution)/shard_map/all_to_all | solution.py:91
  154.1 5.7 %reduce-scatter.8.cloned.1.call-done = bf16[1,8,512]{2,1,0:T(8,128)(2,1)} async-done(((bf16[1,32,512]{2,1,0:T(8,128)(2,1)}), bf16[1,8,512]{2,1,0:T(8,128)(2,1)}) %reduce-scatter.8.cloned.1.call-update) | async-done | bytes 8208 | tf_op jit(solution)/shard_map/reduce_scatter | solution.py:98
  159.8 1.3 convert_element_type.68
  161.1 22.9 %reduce-scatter.6.cloned.1.call-done = bf16[1,32,2048]{2,1,0:T(8,128)(2,1)} async-done(((bf16[1,32,8192]{2,1,0:T(8,128)(2,1)}), bf16[1,32,2048]{2,1,0:T(8,128)(2,1)}) %reduce-scatter.6.cloned.1.call-update) | async-done | bytes 131088 | tf_op jit(solution)/shard_map/reduce_scatter | solution.py:95
  184.0 1.6 convert_element_type.65
  185.6 0.1 convert_reduce_fusion
  185.7 64.8 %reduce-scatter.4.cloned.1.call-done = bf16[96,512]{1,0:T(8,128)(2,1)} async-done(((bf16[768,512]{1,0:T(8,128)(2,1)}), bf16[96,512]{1,0:T(8,128)(2,1)}) %reduce-scatter.4.cloned.1.call-update) | async-done | bytes 98320 | tf_op jit(solution)/shard_map/reduce_scatter | solution.py:78
  250.5 1.6 add_convert_fusion
  (19 shorter events, 0.2 us)
Async XLA Ops:
  7.2 138.4 %copy-start = (bf16[1024,512]{1,0:T(8,128)(2,1)S(1)}, bf16[1024,512]{1,0:T(8,128)(2,1)}, u32[]{:S(2)}) copy-start(bf16[1024,512]{1,0:T(8,128)(2,1)} %param.8) | copy-start | bytes 3145732
  26.8 7.4 %copy-start.4 = (bf16[768,64]{0,1:T(8,128)(2,1)S(1)}, bf16[768,64]{0,1:T(8,128)(2,1)}, u32[]{:S(2)}) copy-start(bf16[768,64]{0,1:T(8,128)(2,1)} %param.7) | copy-start | bytes 294916
  26.8 104.4 %copy-start.2 = (bf16[1,32,8192]{2,1,0:T(8,128)(2,1)S(1)}, bf16[1,32,8192]{2,1,0:T(8,128)(2,1)}, u32[]{:S(2)}) copy-start(bf16[1,32,8192]{2,1,0:T(8,128)(2,1)} %param.9) | copy-start | bytes 1572868
  26.8 100.7 %all-to-all-start = ((bf16[8,256,1024]{1,2,0:T(8,128)(2,1)}), bf16[8,256,1024]{1,2,0:T(8,128)(2,1)}, u32[]{:S(2)}, u32[]{:S(2)}) async-start(bf16[8,256,1024]{1,2,0:T(8,128)(2,1)} %copy.15), calls=%async_computation.1 | async-start | bytes 8388608 | tf_op jit(solution)/shard_map/all_to_all | solution.py:53
  34.2 106.9 %copy-start.3 = (bf16[1,32,512]{2,1,0:T(8,128)(2,1)S(1)}, bf16[1,32,512]{2,1,0:T(8,128)(2,1)}, u32[]{:S(2)}) copy-start(bf16[1,32,512]{2,1,0:T(8,128)(2,1)} %param.10) | copy-start | bytes 98308
  127.5 12.7 %all-to-all-start.2 = ((bf16[8,256,64]{1,2,0:T(8,128)(2,1)}), bf16[8,256,64]{1,2,0:T(8,128)(2,1)S(1)}, u32[]{:S(2)}, u32[]{:S(2)}) async-start(bf16[8,256,64]{1,2,0:T(8,128)(2,1)} %copy.17), calls=%async_computation.3 | async-start | bytes 524288 | tf_op jit(solution)/shard_map/all_to_all | solution.py:54
  131.1 28.7 %reduce-scatter.8.cloned.1.call-start = ((), (), s32[]{:S(2)}) async-start(), calls=%async_computation.8 | async-start | bytes 40960 | tf_op jit(solution)/shard_map/reduce_scatter | solution.py:98
  131.2 14.4 %copy-start.1 = (bf16[768,1024]{1,0:T(8,128)(2,1)S(1)}, bf16[768,1024]{1,0:T(8,128)(2,1)}, u32[]{:S(2)}) copy-start(bf16[768,1024]{1,0:T(8,128)(2,1)} %param.6) | copy-start | bytes 4718596
  141.0 43.0 %reduce-scatter.6.cloned.1.call-start = ((), (), s32[]{:S(2)}) async-start(), calls=%async_computation.7 | async-start | bytes 655360 | tf_op jit(solution)/shard_map/reduce_scatter | solution.py:95
  145.5 105.0 %reduce-scatter.4.cloned.1.call-start = ((), (), s32[]{:S(2)}) async-start(), calls=%async_computation.6 | async-start | bytes 884736 | tf_op jit(solution)/shard_map/reduce_scatter | solution.py:78
  150.5 35.1 %all-to-all-start.1 = ((bf16[8,96,512]{2,1,0:T(8,128)(2,1)}), bf16[8,96,512]{2,1,0:T(8,128)(2,1)S(1)}, u32[]{:S(2)}, u32[]{:S(2)}) async-start(bf16[8,96,512]{2,1,0:T(8,128)(2,1)} %reshape.98), calls=%async_computation.2 | async-start | bytes 1572864 | tf_op jit(solution)/shard_map/all_to_all | solution.py:91
Sparse Core Ops, SparseCore 0:
  141.2 18.5 reduce-scatter.7
  162.3 21.6 reduce-scatter.5
  187.3 63.1 reduce-scatter.3
where the time goes:
time: 259 us
  waiting for transfers between devices  191 us (74%)
  local copies, waits for them, and re-layouts  18.8 us (7%)
  starting transfers between devices  14.8 us (6%)
  matrix products  14.4 us (6%)
  between operations  13.9 us (5%)
  other arithmetic  6.27 us (2%)
    all_to_all x1, waiting for transfers between devices, shards(): lax.all_to_all(send_tokens, 'tensor', split_axis=0, concat_axis=2, tiled=...  91.2 us
    reduce_scatter x1, waiting for transfers between devices, shards(): lax.psum_scatter(jnp.dot(tokens, frozen_value_weight, preferred_element_t...  64.8 us
    reduce_scatter x1, waiting for transfers between devices, shards(): lax.psum_scatter(local_down[None].astype(jnp.bfloat16), 'dp', scatter_dim...  22.9 us
    reshape x2, local copies, waits for them, and re-layouts, shards(): send_tokens = send_tokens.reshape(tensor_size, CAP * BLK, feature_width)  11.3 us
    all_to_all x1, starting transfers between devices, shards(): lax.all_to_all(send_tokens, 'tensor', split_axis=0, concat_axis=2, tiled=...  7.41 us
    all_to_all x1, waiting for transfers between devices, shards(): lax.all_to_all(send_cot, 'tensor', split_axis=0, concat_axis=2, tiled=True)  5.91 us
    reduce_scatter x1, waiting for transfers between devices, shards(): lax.psum_scatter(member_up_weight[None].astype(jnp.bfloat16), 'dp', scatt...  5.65 us
  transfers between devices with their start and end apart: 6, of which 5 were waited for; matrix products, arithmetic and copies ran while one was open for 7% of the time, Pallas kernels for 0%

commit v1 on v0

v1 whole, which is shorter than its diff:
```python
import functools

import jax
import jax.numpy as jnp
from jax import lax
from jax.experimental import pallas as pl
from jax.experimental.pallas import tpu as pltpu
from jax.sharding import PartitionSpec as P

BLK = 128
SCALE = 2.0
TRAIL = (((1,), (1,)), ((), ()))
LEAD = (((0,), (0,)), ((), ()))
F32 = jnp.float32
BF16 = jnp.bfloat16


def kernel(n, dp, member, tok, cot, w, down, up, out, gdown, gup, dw, uw, ms, mr, hb, gs, gr, us, ur,
           wd_s, wd_r, wu_s, wu_r, fd_s, fd_r, fu_s, fu_r, m_s, m_r, h_s, h_r, g_s, g_r, u_s, u_r):
    d = lax.axis_index("dp")
    j = lax.axis_index("tensor")
    total = dp * n
    lin = d * n + j
    _, rows, feat = tok.shape
    cw = cot.shape[2]
    rank, width = up.shape
    half = rank // 2
    per = n // dp
    core = d % 2
    mate = d + 1 - 2 * core
    blocks = member.shape[0]
    mine = pl.ds(pl.multiple_of(core * half, half), half)
    other = pl.ds(pl.multiple_of((1 - core) * half, half), half)

    def rcopy(src, dst, s, r, dd, tt):
        return pltpu.make_async_remote_copy(
            src_ref=src, dst_ref=dst, send_sem=s, recv_sem=r,
            device_id={"dp": dd, "tensor": tt}, device_id_type=pl.DeviceIdType.MESH)

    def loop(lo, hi, fn):
        def step(k, c):
            fn(k)
            return c
        lax.fori_loop(lo, hi, step, 0)

    barrier = pltpu.get_barrier_semaphore()

    def greet(o):
        t = (lin + o) % total
        pl.semaphore_signal(barrier, inc=1, device_id={"dp": t // n, "tensor": t % n},
                            device_id_type=pl.DeviceIdType.MESH)

    loop(1, total, greet)
    dw[j] = down[:, pl.ds(pl.multiple_of(j * feat, feat), feat)]
    uw[j] = up[...]
    pl.semaphore_wait(barrier, total - 1)

    def down_copy(o):
        t = (j + o) % n
        return rcopy(down.at[mine, pl.ds(pl.multiple_of(t * feat, feat), feat)], dw.at[j, mine],
                     wd_s.at[o], wd_r.at[o], d, t)

    def up_copy(o):
        t = (j + o) % n
        return rcopy(up.at[mine], uw.at[j, mine], wu_s.at[o], wu_r.at[o], d, t)

    loop(1, n, lambda o: down_copy(o).start())
    loop(1, n, lambda o: up_copy(o).start())

    def base(i):
        ms[i, :, 0:width] = jnp.dot(tok[i], w[...], preferred_element_type=F32).astype(BF16)

    loop(0, n, base)

    def fdown(o, part):
        s = (j + n - o) % n
        return rcopy(dw.at[s, part], dw.at[s, part], fd_s.at[o], fd_r.at[o], mate, j)

    def fup(o, part):
        s = (j + n - o) % n
        return rcopy(uw.at[s, part], uw.at[s, part], fu_s.at[o], fu_r.at[o], mate, j)

    def got_down(o):
        s = (j + n - o) % n
        rcopy(dw.at[s, mine], dw.at[s, mine], wd_s.at[o], wd_r.at[o], d, s).wait_recv()
        fdown(o, mine).start()

    def got_up(o):
        s = (j + n - o) % n
        rcopy(uw.at[s, mine], uw.at[s, mine], wu_s.at[o], wu_r.at[o], d, s).wait_recv()
        fup(o, mine).start()

    loop(1, n, got_down)
    loop(1, n, got_up)
    loop(1, n, lambda o: fdown(o, other).wait_recv())
    loop(1, n, lambda o: fup(o, other).wait_recv())

    pick = (lax.broadcasted_iota(jnp.int32, (width, cw), 0)
            == lax.broadcasted_iota(jnp.int32, (width, cw), 1) + j * cw).astype(BF16)

    def owners(i):
        k0 = (i * rows) // BLK
        k1 = (i * rows + rows - 1) // BLK
        return member[k0], member[k1], (k0 + 1) * BLK - i * rows

    def msg(i, o):
        return rcopy(ms.at[i], mr.at[j], m_s.at[o], m_r.at[o], d, i)

    def split(x):
        hi = x.astype(BF16)
        return hi, (x - hi.astype(F32)).astype(BF16)

    def partial(o):
        i = (j + o) % n
        m0, m1, edge = owners(i)
        first = lax.broadcasted_iota(jnp.int32, (rows, rank), 0) < edge
        pair = jnp.concatenate([dw[m0], dw[m1]], axis=0)
        hs = lax.dot_general(tok[i], pair, TRAIL, preferred_element_type=F32)
        upair = jnp.concatenate([uw[m0], uw[m1]], axis=0)
        uj = jnp.dot(upair, pick, preferred_element_type=F32).astype(BF16)
        bs = SCALE * lax.dot_general(cot[i], uj, TRAIL, preferred_element_type=F32)
        h = jnp.where(first, hs[:, :rank], hs[:, rank:])
        b = jnp.where(first, bs[:, :rank], bs[:, rank:])
        ms[i, :, width:] = jnp.concatenate([*split(h), *split(b)], axis=1)

    def partial_send(o):
        partial(o)
        msg((j + o) % n, o).start()

    loop(1, n, partial_send)
    partial(0)

    def msg_recv(o):
        s = (j + n - o) % n
        rcopy(mr.at[s], mr.at[s], m_s.at[o], m_r.at[o], d, s).wait_recv()

    loop(1, n, msg_recv)
    mr[j] = ms[j]
    side = sum(mr[s, :, width:].astype(F32) for s in range(n))
    hidden = (side[:, :rank] + side[:, rank:2 * rank]).astype(BF16)
    back = (side[:, 2 * rank:3 * rank] + side[:, 3 * rank:]).astype(BF16)
    hb[j] = jnp.concatenate([hidden, back], axis=1)

    def hb_copy(o):
        return rcopy(hb.at[j], hb.at[j], h_s.at[o], h_r.at[o], d, (j + o) % n)

    loop(1, n, lambda o: hb_copy(o).start())

    m0, m1, edge = owners(j)
    a0 = SCALE * jnp.dot(hidden, uw[m0], preferred_element_type=F32)
    a1 = SCALE * jnp.dot(hidden, uw[m1], preferred_element_type=F32)
    first = lax.broadcasted_iota(jnp.int32, (rows, width), 0) < edge
    adapter = jnp.where(first, a0, a1).astype(BF16).astype(F32)
    base_total = sum(mr[s, :, :width].astype(F32) for s in range(n))
    out[...] = (base_total + adapter).astype(BF16)

    def hb_recv(o):
        s = (j + n - o) % n
        rcopy(hb.at[s], hb.at[s], h_s.at[o], h_r.at[o], d, s).wait_recv()

    loop(1, n, hb_recv)

    def flat(x):
        if rows % 16 == 0:
            return x.reshape(n * rows, x.shape[2])
        return x.astype(F32).reshape(n * rows, x.shape[2]).astype(BF16)

    both = flat(hb[...])
    span = n * rank
    row_block = lax.broadcasted_iota(jnp.int32, (n * rows, 1), 0) // BLK
    row_member = jnp.zeros((n * rows, 1), jnp.int32)
    for k in range(blocks):
        row_member = jnp.where(row_block == k, member[k], row_member)
    keep = lax.broadcasted_iota(jnp.int32, (n * rows, span), 1) // rank == row_member
    ra = lax.broadcasted_iota(jnp.int32, (2 * rank, span), 0)
    rb = lax.broadcasted_iota(jnp.int32, (2 * rank, span), 1) % rank

    def spread(offset):
        tiled = jnp.dot(both, (ra == rb + offset).astype(BF16), preferred_element_type=F32)
        return jnp.where(keep, tiled, 0.0).astype(BF16)

    gd = lax.dot_general(spread(rank), flat(tok[...]), LEAD, preferred_element_type=F32)
    gs[...] = gd.astype(BF16).reshape(n, rank, feat)

    dd, slot = j // per, d * per + j % per

    def gd_copy(m):
        return rcopy(gs.at[m], gr.at[slot], g_s.at[m], g_r.at[slot], dd, m)

    def not_me(m):
        return jnp.logical_or(dd != d, m != j)

    def gd_start(m):
        @pl.when(not_me(m))
        def _():
            gd_copy(m).start()

    loop(0, n, gd_start)

    @pl.when(dd == d)
    def _():
        gr[slot] = gs[j]

    gu = (SCALE * lax.dot_general(spread(0), flat(cot[...]), LEAD, preferred_element_type=F32))
    gu = gu.reshape(n, rank, cw)
    part = rank // dp
    for k in range(dp):
        us[:, k] = gu[:, k * part:(k + 1) * part, :]

    def gu_copy(o):
        t = (lin + o) % total
        return rcopy(us.at[t % n, t // n], ur.at[d, j], u_s.at[o], u_r.at[o], t // n, t % n)

    loop(1, total, lambda o: gu_copy(o).start())
    ur[d, j] = us[j, d]

    def gd_recv(k):
        sd, sj = k // per, d * per + k % per

        @pl.when(jnp.logical_or(sd != d, sj != j))
        def _():
            rcopy(gr.at[k], gr.at[k], g_s.at[0], g_r.at[k], sd, sj).wait_recv()

    loop(0, dp * per, gd_recv)
    for q in range(per):
        gdown[:, q * feat:(q + 1) * feat] = sum(gr[k * per + q].astype(F32) for k in range(dp))

    def gu_recv(o):
        s = (lin + total - o) % total
        rcopy(ur.at[s // n, s % n], ur.at[s // n, s % n], u_s.at[o], u_r.at[o], s // n, s % n).wait_recv()

    loop(1, total, gu_recv)
    gup[...] = jnp.concatenate([sum(ur[k, t] for k in range(dp)) for t in range(n)], axis=1)

    def drain(o):
        down_copy(o).wait_send()
        up_copy(o).wait_send()
        fdown(o, mine).wait_send()
        fup(o, mine).wait_send()
        msg((j + o) % n, o).wait_send()
        hb_copy(o).wait_send()

    loop(1, n, drain)

    def gd_drain(m):
        @pl.when(not_me(m))
        def _():
            gd_copy(m).wait_send()

    loop(0, n, gd_drain)
    loop(1, total, lambda o: gu_copy(o).wait_send())


def solution(mesh):
    dp, n = mesh.shape["dp"], mesh.shape["tensor"]

    def shards(tokens, cotangent, w, down, up, member):
        rows, feat = tokens.shape[0] // n, tokens.shape[1]
        cw, width, rank = cotangent.shape[1], w.shape[1], up.shape[1]
        per = n // dp
        vmem = pl.BlockSpec(memory_space=pltpu.VMEM)
        dma = lambda k: pltpu.SemaphoreType.DMA((k,))
        out, gdown, gup = pl.pallas_call(
            functools.partial(kernel, n, dp),
            out_shape=(
                jax.ShapeDtypeStruct((rows, width), BF16),
                jax.ShapeDtypeStruct((rank, per * feat), F32),
                jax.ShapeDtypeStruct((rank // dp, width), F32),
            ),
            in_specs=[pl.BlockSpec(memory_space=pltpu.SMEM)] + [vmem] * 5,
            out_specs=(vmem,) * 3,
            scratch_shapes=[
                pltpu.VMEM((n, rank, feat), BF16),
                pltpu.VMEM((n, rank, width), BF16),
                pltpu.VMEM((n, rows, width + 4 * rank), BF16),
                pltpu.VMEM((n, rows, width + 4 * rank), BF16),
                pltpu.VMEM((n, rows, 2 * rank), BF16),
                pltpu.VMEM((n, rank, feat), BF16),
                pltpu.VMEM((dp * per, rank, feat), BF16),
                pltpu.VMEM((n, dp, rank // dp, cw), F32),
                pltpu.VMEM((dp, n, rank // dp, cw), F32),
                *[dma(n) for _ in range(12)],
                dma(n), dma(dp * per), dma(dp * n), dma(dp * n),
            ],
            compiler_params=pltpu.CompilerParams(
                collective_id=0, has_side_effects=True, vmem_limit_bytes=62 * 1024 * 1024),
        )(member[:, 0], tokens.reshape(n, rows, feat), cotangent.reshape(n, rows, cw), w, down[0], up[0])
        return out, gdown[None], gup[None]

    return jax.shard_map(
        shards,
        mesh=mesh,
        in_specs=(P("dp", "tensor"), P("dp", "tensor"), P("tensor", None), P("tensor", None, None),
                  P("tensor", None, None), P("dp", None)),
        out_specs=(P(("dp", "tensor"), None), P("tensor", None, "dp"), P("tensor", "dp", None)),
        check_vma=False,
    )
```

time: 259 us -> 77.7 us (0.30)
  waiting for transfers between devices: 191 us -> 0 us
  Pallas kernels: 0 us -> 70.6 us
  starting transfers between devices: 14.8 us -> 0 us
  matrix products: 14.4 us -> 0 us
  between operations: 13.9 us -> 0.64 us
  local copies, waits for them, and re-layouts: 18.8 us -> 6.24 us
  other arithmetic: 6.27 us -> 0 us
    all_to_all x3 -> x0, waiting for transfers between devices: 97.2 us -> none  [the longest x1 91.2 us: shards(): lax.all_to_all(send_tokens, 'tensor', split_axis=0, concat_axis=2, tiled=...]
    reduce_scatter x3 -> x0, waiting for transfers between devices: 93.4 us -> none  [the longest x1 64.8 us: shards(): lax.psum_scatter(jnp.dot(tokens, frozen_value_weight, preferred_element_t...]
    pallas_call x0 -> x1, Pallas kernels: none -> 70.6 us  [shards(): pl.pallas_call(functools.partial(kernel, n, dp), out_shape=(jax.ShapeDtyp...]
    reshape x8 -> x0, local copies, waits for them, and re-layouts: 18.6 us -> none  [the longest x2 11.3 us: shards(): send_tokens = send_tokens.reshape(tensor_size, CAP * BLK, feature_width)]
    all_to_all x3 -> x0, starting transfers between devices: 14.6 us -> none  [the longest x1 7.41 us: shards(): lax.all_to_all(send_tokens, 'tensor', split_axis=0, concat_axis=2, tiled=...]
    dot_general x8 -> x0, matrix products: 14.4 us -> none  [the longest x1 4.4 us: shards(): lax.dot_general(backward_projection, slot_tokens, contract_leading, prefe...]
    unnamed x11 -> x4, local copies, waits for them, and re-layouts: 0.19 us -> 6.24 us
    convert_element_type x3 -> x0, other arithmetic: 4.48 us -> none  [the longest x2 2.93 us: shards(): grad_down, grad_up = (lax.psum_scatter(local_down[None].astype(jnp.bfloat...]
  transfers between devices with their start and end apart: 6 -> 0, of which waited for: 5 -> 0; matrix products, arithmetic and copies ran while one was open for 7% -> 0% of each run, Pallas kernels for 0% -> 0%
where the time goes in v1:
time: 77.7 us; the launch traced here: 77.4 us
  Pallas kernels  70.6 us (91%)
  local copies, waits for them, and re-layouts  6.24 us (8%)
    pallas_call x1, Pallas kernels, shards(): pl.pallas_call(functools.partial(kernel, n, dp), out_shape=(jax.ShapeDtyp...  70.6 us
    unnamed x4, local copies, waits for them, and re-layouts  6.24 us

profile of v1, /device:TPU:0, one launch (start us, length us, event | category | flops | bytes accessed | tf_op | source)
XLA Modules:
  0.0 77.4 jit_solution(5406057630821475891)
XLA Ops:
  0.6 1.7 %copy.9 = bf16[768,64]{1,0:T(8,128)(2,1)} copy(bf16[768,64]{0,1:T(8,128)(2,1)} %param.7) | data formatting | bytes 196608 | tf_op args[1]
  2.3 70.6 %shard_map.85 = (bf16[96,512]{1,0:T(8,128)(2,1)}, f32[32,2048]{1,0:T(8,128)}, f32[8,512]{1,0:T(8,128)}) custom-call(s32[6]{0:T(128)} %bitcast.13, bf16[8,96,1024]{2,1,0:T(8,128)(2,1)} %bitcast.7, bf16[8,96,64]{2,1,0:T(8,128)(2,1)} %bitcast.8, bf16[1024,512]{1,0:T(8,128)(2,1)} %w.1, bf16[32,8192]{1,0:T(8,128)(2,1)} %bitcast.9, bf16[32,512]{1,0:T(8,128)(2,1)} %bitcast.11), custom_call_target="tpu_custom_call" | custom-call | tf_op jit(solution)/shard_map/pallas_call | solution.py:263
  72.9 1.5 %copy.13 = bf16[96,512]{1,0:T(8,128)(2,1)} copy(bf16[96,512]{1,0:T(8,128)(2,1)} %get-tuple-element.12) | data formatting | bytes 196608
  74.4 1.7 %copy.14 = f32[1,32,2048]{2,1,0:T(8,128)} copy(f32[1,32,2048]{2,1,0:T(8,128)} %bitcast.10) | data formatting | bytes 524288
  76.1 1.3 %copy.15 = f32[1,8,512]{2,1,0:T(8,128)} copy(f32[1,8,512]{2,1,0:T(8,128)} %bitcast.12) | data formatting | bytes 32768

commit v2 on v1

v2 whole, which is shorter than its diff:
```python
import functools

import jax
import jax.numpy as jnp
from jax import lax
from jax.experimental import pallas as pl
from jax.experimental.pallas import tpu as pltpu
from jax.sharding import PartitionSpec as P

BLK = 128
SCALE = 2.0
TRAIL = (((1,), (1,)), ((), ()))
LEAD = (((0,), (0,)), ((), ()))
F32 = jnp.float32
BF16 = jnp.bfloat16


def kernel(n, dp, member, tok_h, cot_h, w_h, down_h, up_h, out, gdown, gup,
           tok, cot_t, w, down, up, cot, dw, uw, bs, bx, br, ss, sx, sr, hb, gs, gx, gr, us, ur,
           in_s, wd_s, wd_r, wu_s, wu_r, fd_s, fd_r, fu_s, fu_r, bx_s, bx_r, bz_s, bz_r,
           sx_s, sx_r, sz_s, sz_r, h_s, h_r, gx_s, gx_r, g_s, g_r, u_s, u_r):
    d = lax.axis_index("dp")
    j = lax.axis_index("tensor")
    total = dp * n
    lin = d * n + j
    _, rows, feat = tok.shape
    cw = cot.shape[2]
    rank, width = up.shape
    half = rank // 2
    per = n // dp
    nz = n // 2
    core = d % 2
    mate = d + 1 - 2 * core
    px = j % 2
    zme = j // 2
    partner = j + 1 - 2 * px
    blocks = member.shape[0]
    mine = pl.ds(pl.multiple_of(core * half, half), half)
    other = pl.ds(pl.multiple_of((1 - core) * half, half), half)

    def rcopy(src, dst, s, r, dd, tt):
        return pltpu.make_async_remote_copy(
            src_ref=src, dst_ref=dst, send_sem=s, recv_sem=r,
            device_id={"dp": dd, "tensor": tt}, device_id_type=pl.DeviceIdType.MESH)

    def loop(lo, hi, fn):
        def step(k, c):
            fn(k)
            return c
        lax.fori_loop(lo, hi, step, 0)

    barrier = pltpu.get_barrier_semaphore()

    def greet(o):
        t = (lin + o) % total
        pl.semaphore_signal(barrier, inc=1, device_id={"dp": t // n, "tensor": t % n},
                            device_id_type=pl.DeviceIdType.MESH)

    loads = [pltpu.make_async_copy(a, b, in_s.at[k]) for k, (a, b) in enumerate(
        ((down_h, down), (up_h, up), (w_h, w), (tok_h, tok), (cot_h, cot_t)))]
    for one in loads:
        one.start()
    loop(1, total, greet)
    for one in loads:
        one.wait()
    dw[j] = down[:, pl.ds(pl.multiple_of(j * feat, feat), feat)]
    uw[j] = up[...]

    def base(i):
        bs[i] = jnp.dot(tok[i], w[...], preferred_element_type=F32).astype(BF16)

    loop(0, nz, lambda z: base(2 * z + 1 - px))
    pl.semaphore_wait(barrier, total - 1)

    def down_copy(o):
        t = (j + o) % n
        return rcopy(down.at[mine, pl.ds(pl.multiple_of(t * feat, feat), feat)], dw.at[j, mine],
                     wd_s.at[o], wd_r.at[o], d, t)

    def up_copy(o):
        t = (j + o) % n
        return rcopy(up.at[mine], uw.at[j, mine], wu_s.at[o], wu_r.at[o], d, t)

    def bx_copy(z):
        return rcopy(bs.at[2 * z + 1 - px], bx.at[z], bx_s.at[z], bx_r.at[z], d, partner)

    loop(1, n, lambda o: down_copy(o).start())
    loop(1, n, lambda o: up_copy(o).start())
    loop(0, nz, lambda z: bx_copy(z).start())
    loop(0, nz, lambda z: base(2 * z + px))

    if rows % 16 == 0:
        cot[...] = cot_t[...].T.reshape(n, rows, cw)
    else:
        cot[...] = cot_t[...].astype(F32).T.reshape(n, rows, cw).astype(BF16)

    def fdown(o, part):
        s = (j + n - o) % n
        return rcopy(dw.at[s, part], dw.at[s, part], fd_s.at[o], fd_r.at[o], mate, j)

    def fup(o, part):
        s = (j + n - o) % n
        return rcopy(uw.at[s, part], uw.at[s, part], fu_s.at[o], fu_r.at[o], mate, j)

    def got_down(o):
        s = (j + n - o) % n
        rcopy(dw.at[s, mine], dw.at[s, mine], wd_s.at[o], wd_r.at[o], d, s).wait_recv()
        fdown(o, mine).start()

    def got_up(o):
        s = (j + n - o) % n
        rcopy(uw.at[s, mine], uw.at[s, mine], wu_s.at[o], wu_r.at[o], d, s).wait_recv()
        fup(o, mine).start()

    loop(1, n, got_down)
    loop(1, n, got_up)

    def z_copy(ref, dst, s_sem, r_sem, o):
        t = 2 * ((zme + o) % nz) + px
        return rcopy(ref.at[t], dst.at[zme], s_sem.at[o], r_sem.at[o], d, t)

    def z_wait(dst, s_sem, r_sem, o):
        s = (zme + nz - o) % nz
        rcopy(dst.at[s], dst.at[s], s_sem.at[o], r_sem.at[o], d, 2 * s + px).wait_recv()

    def base_join(o):
        z = (zme + o) % nz
        bx_copy(z).wait_recv()
        i = 2 * z + px
        bs[i] = (bs[i].astype(F32) + bx[z].astype(F32)).astype(BF16)

    def base_send(o):
        base_join(o)
        z_copy(bs, br, bz_s, bz_r, o).start()

    loop(1, nz, base_send)
    base_join(0)

    loop(1, n, lambda o: fdown(o, other).wait_recv())
    loop(1, n, lambda o: fup(o, other).wait_recv())

    pick = (lax.broadcasted_iota(jnp.int32, (width, cw), 0)
            == lax.broadcasted_iota(jnp.int32, (width, cw), 1) + j * cw).astype(BF16)

    def owners(i):
        k0 = (i * rows) // BLK
        k1 = (i * rows + rows - 1) // BLK
        return member[k0], member[k1], (k0 + 1) * BLK - i * rows

    def split(x):
        hi = x.astype(BF16)
        return hi, (x - hi.astype(F32)).astype(BF16)

    def partial(i):
        m0, m1, edge = owners(i)
        first = lax.broadcasted_iota(jnp.int32, (rows, rank), 0) < edge
        pair = jnp.concatenate([dw[m0], dw[m1]], axis=0)
        hs = lax.dot_general(tok[i], pair, TRAIL, preferred_element_type=F32)
        upair = jnp.concatenate([uw[m0], uw[m1]], axis=0)
        uj = jnp.dot(upair, pick, preferred_element_type=F32).astype(BF16)
        cs = SCALE * lax.dot_general(cot[i], uj, TRAIL, preferred_element_type=F32)
        h = jnp.where(first, hs[:, :rank], hs[:, rank:])
        b = jnp.where(first, cs[:, :rank], cs[:, rank:])
        ss[i] = jnp.concatenate([*split(h), *split(b)], axis=1)

    def merged(x):
        return (x[:, :rank] + x[:, rank:2 * rank], x[:, 2 * rank:3 * rank] + x[:, 3 * rank:])

    def sx_copy(z):
        return rcopy(ss.at[2 * z + 1 - px], sx.at[z], sx_s.at[z], sx_r.at[z], d, partner)

    def partial_send(o):
        z = (zme + o) % nz
        partial(2 * z + 1 - px)
        sx_copy(z).start()

    loop(1, nz + 1, partial_send)
    loop(0, nz, lambda z: partial(2 * z + px))

    def side_join(o):
        z = (zme + o) % nz
        sx_copy(z).wait_recv()
        i = 2 * z + px
        h, b = merged(ss[i].astype(F32) + sx[z].astype(F32))
        ss[i] = jnp.concatenate([*split(h), *split(b)], axis=1)

    def side_send(o):
        side_join(o)
        z_copy(ss, sr, sz_s, sz_r, o).start()

    loop(1, nz, side_send)
    side_join(0)
    sr[zme] = ss[j]
    loop(1, nz, lambda o: z_wait(sr, sz_s, sz_r, o))
    hidden, back = merged(sum(sr[s].astype(F32) for s in range(nz)))
    hidden, back = hidden.astype(BF16), back.astype(BF16)
    hb[j] = jnp.concatenate([hidden, back], axis=1)

    def hb_copy(o):
        return rcopy(hb.at[j], hb.at[j], h_s.at[o], h_r.at[o], d, (j + o) % n)

    loop(1, n, lambda o: hb_copy(o).start())

    def flat(x):
        if rows % 16 == 0:
            return x.reshape(n * rows, x.shape[2])
        return x.astype(F32).reshape(n * rows, x.shape[2]).astype(BF16)

    span = n * rank
    row_block = lax.broadcasted_iota(jnp.int32, (n * rows, 1), 0) // BLK
    row_member = jnp.zeros((n * rows, 1), jnp.int32)
    for k in range(blocks):
        row_member = jnp.where(row_block == k, member[k], row_member)

    def hb_recv(o):
        s = (j + n - o) % n
        rcopy(hb.at[s], hb.at[s], h_s.at[o], h_r.at[o], d, s).wait_recv()

    loop(1, n, hb_recv)
    both = flat(hb[...])

    def spread(offset, lo, size):
        keep = lax.broadcasted_iota(jnp.int32, (n * rows, size), 1) // rank + lo == row_member
        ra = lax.broadcasted_iota(jnp.int32, (2 * rank, size), 0)
        rb = lax.broadcasted_iota(jnp.int32, (2 * rank, size), 1) % rank
        tiled = jnp.dot(both, (ra == rb + offset).astype(BF16), preferred_element_type=F32)
        return jnp.where(keep, tiled, 0.0).astype(BF16)

    def grads_of(lo):
        g = lax.dot_general(spread(rank, lo, nz * rank), flat(tok[...]), LEAD, preferred_element_type=F32)
        return g.reshape(nz, rank, feat)

    def gx_copy(k):
        return rcopy(gs.at[k], gx.at[k], gx_s.at[k], gx_r.at[k], mate, j)

    gs[0:nz] = grads_of((1 - core) * nz).astype(BF16)
    loop(0, nz, lambda k: gx_copy(k).start())
    gs[nz:n] = grads_of(core * nz).astype(BF16)

    dd, slot = j // per, (d // 2) * per + j % per

    def gd_copy(k):
        return rcopy(gs.at[nz + k], gr.at[slot], g_s.at[k], g_r.at[slot], dd, core * nz + k)

    def not_me(k):
        return jnp.logical_or(dd != d, core * nz + k != j)

    def gd_start(k):
        gx_copy(k).wait_recv()
        gs[nz + k] = (gs[nz + k].astype(F32) + gx[k].astype(F32)).astype(BF16)

        @pl.when(not_me(k))
        def _():
            gd_copy(k).start()

    loop(0, nz, gd_start)

    @pl.when(jnp.logical_and(dd == d, j // nz == core))
    def _():
        gr[slot] = gs[nz + j % nz]

    gu = (SCALE * lax.dot_general(spread(0, 0, span), flat(cot[...]), LEAD, preferred_element_type=F32))
    gu = gu.reshape(n, rank, cw)
    part = rank // dp
    for k in range(dp):
        us[:, k] = gu[:, k * part:(k + 1) * part, :]

    def gu_copy(o):
        t = (lin + o) % total
        return rcopy(us.at[t % n, t // n], ur.at[d, j], u_s.at[o], u_r.at[o], t // n, t % n)

    loop(1, total, lambda o: gu_copy(o).start())
    ur[d, j] = us[j, d]

    m0, m1, edge = owners(j)
    a0 = SCALE * jnp.dot(hidden, uw[m0], preferred_element_type=F32)
    a1 = SCALE * jnp.dot(hidden, uw[m1], preferred_element_type=F32)
    first = lax.broadcasted_iota(jnp.int32, (rows, width), 0) < edge
    adapter = jnp.where(first, a0, a1).astype(BF16).astype(F32)
    br[zme] = bs[j]
    loop(1, nz, lambda o: z_wait(br, bz_s, bz_r, o))
    out[...] = (sum(br[s].astype(F32) for s in range(nz)) + adapter).astype(BF16)

    ny = dp // 2

    def gd_recv(k):
        sd, sj = 2 * (k // per) + j // nz, d * per + k % per

        @pl.when(jnp.logical_or(sd != d, sj != j))
        def _():
            rcopy(gr.at[k], gr.at[k], g_s.at[0], g_r.at[k], sd, sj).wait_recv()

    loop(0, ny * per, gd_recv)
    for q in range(per):
        gdown[:, q * feat:(q + 1) * feat] = sum(gr[k * per + q].astype(F32) for k in range(ny))

    def gu_recv(o):
        s = (lin + total - o) % total
        rcopy(ur.at[s // n, s % n], ur.at[s // n, s % n], u_s.at[o], u_r.at[o], s // n, s % n).wait_recv()

    loop(1, total, gu_recv)
    gup[...] = jnp.concatenate([sum(ur[k, t] for k in range(dp)) for t in range(n)], axis=1)

    def drain(o):
        down_copy(o).wait_send()
        up_copy(o).wait_send()
        fdown(o, mine).wait_send()
        fup(o, mine).wait_send()
        hb_copy(o).wait_send()

    loop(1, n, drain)

    def drain_pair(z):
        bx_copy(z).wait_send()
        sx_copy(z).wait_send()
        gx_copy(z).wait_send()

    loop(0, nz, drain_pair)

    def drain_z(o):
        z_copy(bs, br, bz_s, bz_r, o).wait_send()
        z_copy(ss, sr, sz_s, sz_r, o).wait_send()

    loop(1, nz, drain_z)

    def gd_drain(k):
        @pl.when(not_me(k))
        def _():
            gd_copy(k).wait_send()

    loop(0, nz, gd_drain)
    loop(1, total, lambda o: gu_copy(o).wait_send())


def solution(mesh):
    dp, n = mesh.shape["dp"], mesh.shape["tensor"]

    def shards(tokens, cotangent, w, down, up, member):
        rows, feat = tokens.shape[0] // n, tokens.shape[1]
        cw, width, rank = cotangent.shape[1], w.shape[1], up.shape[1]
        per, nz = n // dp, n // 2
        vmem = pl.BlockSpec(memory_space=pltpu.VMEM)
        dma = lambda k: pltpu.SemaphoreType.DMA((k,))
        out, gdown, gup = pl.pallas_call(
            functools.partial(kernel, n, dp),
            out_shape=(
                jax.ShapeDtypeStruct((rows, width), BF16),
                jax.ShapeDtypeStruct((rank, per * feat), F32),
                jax.ShapeDtypeStruct((rank // dp, width), F32),
            ),
            in_specs=[pl.BlockSpec(memory_space=pltpu.SMEM)] + [pl.BlockSpec(memory_space=pl.ANY)] * 5,
            out_specs=(vmem,) * 3,
            scratch_shapes=[
                pltpu.VMEM((n, rows, feat), BF16),
                pltpu.VMEM((cw, n * rows), BF16),
                pltpu.VMEM((feat, width), BF16),
                pltpu.VMEM((rank, n * feat), BF16),
                pltpu.VMEM((rank, width), BF16),
                pltpu.VMEM((n, rows, cw), BF16),
                pltpu.VMEM((n, rank, feat), BF16),
                pltpu.VMEM((n, rank, width), BF16),
                pltpu.VMEM((n, rows, width), BF16),
                pltpu.VMEM((nz, rows, width), BF16),
                pltpu.VMEM((nz, rows, width), BF16),
                pltpu.VMEM((n, rows, 4 * rank), BF16),
                pltpu.VMEM((nz, rows, 4 * rank), BF16),
                pltpu.VMEM((nz, rows, 4 * rank), BF16),
                pltpu.VMEM((n, rows, 2 * rank), BF16),
                pltpu.VMEM((n, rank, feat), BF16),
                pltpu.VMEM((nz, rank, feat), BF16),
                pltpu.VMEM((dp // 2 * per, rank, feat), BF16),
                pltpu.VMEM((n, dp, rank // dp, cw), F32),
                pltpu.VMEM((dp, n, rank // dp, cw), F32),
                dma(5),
                *[dma(n) for _ in range(8)],
                *[dma(nz) for _ in range(8)],
                dma(n), dma(n), dma(nz), dma(nz), dma(nz), dma(dp // 2 * per),
                dma(dp * n), dma(dp * n),
            ],
            compiler_params=pltpu.CompilerParams(
                collective_id=0, has_side_effects=True, vmem_limit_bytes=62 * 1024 * 1024),
        )(member[:, 0], tokens.reshape(n, rows, feat), cotangent.T, w, down[0], up[0])
        return out, gdown[None], gup[None]

    return jax.shard_map(
        shards,
        mesh=mesh,
        in_specs=(P("dp", "tensor"), P("dp", "tensor"), P("tensor", None), P("tensor", None, None),
                  P("tensor", None, None), P("dp", None)),
        out_specs=(P(("dp", "tensor"), None), P("tensor", None, "dp"), P("tensor", "dp", None)),
        check_vma=False,
    )
```

time: 77.7 us -> 58.7 us (0.76)
  Pallas kernels: 70.6 us -> 53.2 us
  local copies, waits for them, and re-layouts: 6.24 us -> 4.53 us
    pallas_call x1, Pallas kernels: 70.6 us -> 53.2 us  [shards(): pl.pallas_call(functools.partial(kernel, n, dp), out_shape=(jax.ShapeDtyp...]
    unnamed x4 -> x3, local copies, waits for them, and re-layouts: 6.24 us -> 4.53 us
where the time goes in v2:
time: 58.7 us; the launch traced here: 58.4 us
  Pallas kernels  53.2 us (91%)
  local copies, waits for them, and re-layouts  4.53 us (8%)
  between operations  0.64 us (1%)
    pallas_call x1, Pallas kernels, shards(): pl.pallas_call(functools.partial(kernel, n, dp), out_shape=(jax.ShapeDtyp...  53.2 us
    unnamed x3, local copies, waits for them, and re-layouts  4.53 us

profile of v2, /device:TPU:0, one launch (start us, length us, event | category | flops | bytes accessed | tf_op | source)
XLA Modules:
  0.0 58.4 jit_solution(11501069739810268891)
XLA Ops:
  0.6 53.2 %shard_map.85 = (bf16[96,512]{1,0:T(8,128)(2,1)}, f32[32,2048]{1,0:T(8,128)}, f32[8,512]{1,0:T(8,128)}) custom-call(s32[6]{0:T(128)} %bitcast.13, bf16[8,96,1024]{2,1,0:T(8,128)(2,1)} %bitcast.7, bf16[64,768]{1,0:T(8,128)(2,1)} %bitcast.10, bf16[1024,512]{1,0:T(8,128)(2,1)} %w_h.1, bf16[32,8192]{1,0:T(8,128)(2,1)} %bitcast.8, bf16[32,512]{1,0:T(8,128)(2,1)} %bitcast.11), custom_call_target="tpu_custom_call" | custom-call | tf_op jit(solution)/shard_map/pallas_call | solution.py:344
  53.9 1.5 %copy.12 = bf16[96,512]{1,0:T(8,128)(2,1)} copy(bf16[96,512]{1,0:T(8,128)(2,1)} %get-tuple-element.12) | data formatting | bytes 196608
  55.4 1.7 %copy.13 = f32[1,32,2048]{2,1,0:T(8,128)} copy(f32[1,32,2048]{2,1,0:T(8,128)} %bitcast.9) | data formatting | bytes 524288
  57.1 1.3 %copy.14 = f32[1,8,512]{2,1,0:T(8,128)} copy(f32[1,8,512]{2,1,0:T(8,128)} %bitcast.12) | data formatting | bytes 32768
